TPU v7x, 256 devices: a whole 4x4x8 slice. The times are simulated.
256 devices in a mesh: wide: 32 (over z, y), narrow: 8 (over x, core).
Axes of the slice: x: 4, y: 4, z: 8, core: 2. Of those that a mesh axis runs over, the one named last changes fastest.
Arguments:
- blocks: float32 [8192, 8, 64, 64], P(('wide', 'narrow'))
- col_index: int32 [8192, 8], P(('wide', 'narrow')), may hold values from 0 to 8191, as said below
- right_side: float32 [16, 524288], P(None, ('wide', 'narrow')), may hold values from -6 to 6
- start_guess: float32 [16, 524288], P(None, ('wide', 'narrow')), may hold values from -3 to 3
Outputs:
- new_guess: float32 [16, 524288], P(None, ('wide', 'narrow'))
- new_residual: float32 [16, 524288], P(None, ('wide', 'narrow'))
Inputs may be any that keep to these rules, and one draw needn't show every extreme that they name: col_index[g, 0] = g; the other entries of row g are distinct and differ from g, each at most 8 block rows away from g counted circularly over 8192 block rows.
All inputs are finite; a program needn't handle non-finite values.
Results may differ from a plain program's by a relative error of at most 0.0003.
Values sent between devices are 32-bit elements; how exact they have to be, the bound alone decides.
A program may use at most 64 MiB of HBM per device.

v0:
```python
import jax
import jax.numpy as jnp
from jax import lax
from jax.sharding import Mesh
from jax.sharding import PartitionSpec as P

S = 4
BAND = 8
WIDE_NARROW = ("wide_0", "wide_1", "narrow_0", "narrow_1")


def with_halo(array, sides, width):
    edges = {}
    for axis, dim in sides:
        peers, length = (lax.axis_size(axis), array.shape[dim])
        up = [(i, (i + 1) % peers) for i in range(peers)]
        last = lax.slice_in_dim(array, length - width, length, axis=dim)
        first = lax.slice_in_dim(array, 0, width, axis=dim)
        edges[dim] = (
            lax.ppermute(last, axis, up),
            lax.ppermute(first, axis, [(b, a) for a, b in up]),
        )
    done = []
    for _, dim in sides:
        low, high = edges[dim]
        around = [(width, width) if d in done else (0, 0) for d in range(array.ndim)]
        array = jnp.concatenate([jnp.pad(low, around), array, jnp.pad(high, around)], axis=dim)
        done.append(dim)
    return array


def one_axis_at_a_time(array, axes):
    for axis in axes:
        array = lax.psum(array, axis)
    return array


def extend_vector(vec, rows):
    cells = vec.shape[1] // rows
    depth = BAND
    extended = with_halo(vec, ((WIDE_NARROW, 1),), BAND * cells)
    return (extended, depth)


def apply_matrix(vec, blocks, col_index):
    rows = blocks.shape[0]
    cells = blocks.shape[2]
    nrhs = vec.shape[0]
    extended, depth = extend_vector(vec, rows)
    total_rows = rows * lax.axis_size(WIDE_NARROW)
    first_row = lax.axis_index(WIDE_NARROW) * rows
    relative = (col_index - first_row + BAND + total_rows) % total_rows
    position = relative - BAND + depth
    shaped = extended.reshape(nrhs, extended.shape[1] // cells, cells)
    picked = jnp.take(shaped, position, axis=1)
    result = jnp.einsum("irkb,rkab->ira", picked, blocks, precision=lax.Precision.HIGHEST)
    return result.reshape(nrhs, rows * cells)


def per_device(blocks, col_index, right_side, start_guess):
    hp = lax.Precision.HIGHEST
    nrhs = right_side.shape[0]
    residual = right_side - apply_matrix(start_guess, blocks, col_index)
    vectors = [residual]
    for step in range(S - 1):
        vectors.append(apply_matrix(vectors[-1], blocks, col_index) - 2.0 * vectors[-1])
    basis = jnp.concatenate(vectors, axis=0)
    local_gram = jnp.dot(basis, basis.T, precision=hp)
    gram = one_axis_at_a_time(local_gram, WIDE_NARROW)
    upper = jnp.linalg.cholesky(gram).T
    lower_cols = (S - 1) * nrhs
    hess = upper[:, nrhs:] + 2.0 * upper[:, :lower_cols]
    normal = jnp.dot(hess.T, hess, precision=hp)
    target = jnp.dot(hess.T, upper[:, :nrhs], precision=hp)
    factor = jnp.linalg.cholesky(normal)
    middle = lax.linalg.triangular_solve(factor, target, left_side=True, lower=True)
    coeff = lax.linalg.triangular_solve(
        factor, middle, left_side=True, lower=True, transpose_a=True
    )
    low_part = basis[:lower_cols]
    high_part = basis[nrhs:] + 2.0 * low_part
    new_guess = start_guess + jnp.dot(coeff.T, low_part, precision=hp)
    new_residual = residual - jnp.dot(coeff.T, high_part, precision=hp)
    return (new_guess, new_residual)


def solution(mesh):
    torus = Mesh(mesh.devices.reshape(8, 4, 4, 2), ("wide_0", "wide_1", "narrow_0", "narrow_1"))
    in_specs = (
        P(WIDE_NARROW, None, None, None),
        P(WIDE_NARROW, None),
        P(None, WIDE_NARROW),
        P(None, WIDE_NARROW),
    )
    out_specs = (P(None, WIDE_NARROW), P(None, WIDE_NARROW))
    return jax.shard_map(
        per_device, mesh=torus, in_specs=in_specs, out_specs=out_specs, check_vma=False
    )
```

profile of v0, /device:TPU:1, one launch (start us, length us, event | category | flops | bytes accessed | tf_op | source)
XLA Modules:
  0.0 166.4 jit_solution(17623749729161626469)
XLA Ops:
  0.6 0.8 fusion.73
  1.4 2.6 %collective-permute-start = (f32[16,512]{1,0:T(8,128)S(1)}, f32[16,512]{1,0:T(8,128)S(1)}, u32[]{:S(2)}, u32[]{:S(2)}) collective-permute-start(f32[16,512]{1,0:T(8,128)S(1)} %get-tuple-element.11), channel_id=1, source_target_pairs={{0,1},{1,2},{2,3},{3,4},{4,5},{5,6},{6,7},{7,8},{8,9},{9,10},{10,1... | collective-permute-start | bytes 98312 | tf_op jit(solution)/shard_map/ppermute | solution.py:20
  4.0 0.7 collective-permute-start.1
  4.7 0.7 compare_and_fusion
  5.7 1.6 collective-permute-done.1
  7.4 0.9 pad_maximum_fusion.3
  8.3 0.1 reshape.49
  8.4 0.1 copy.37
  8.5 1.0 gather_fusion
  9.6 9.4 %fusion.12 = f32[16,32,64]{2,0,1:T(8,128)S(1)} fusion(f32[32,8,64,64]{3,2,1,0:T(8,128)} %param.6, f32[32,8,16,64]{3,2,1,0:T(8,128)S(1)} %bitcast.70, pred[32,8]{1,0:T(8,128)(4,1)S(1)} %copy.35), kind=kOutput, calls=%fused_computation.18 | convolution fusion | flops 201588736 | bytes 5374208 | tf_op jit(solution)/shard_map/irkb,rkab->ira/dot_general | solution.py:56
  19.3 7.3 %collective-permute-start.3 = (f32[16,512]{1,0:T(8,128)S(1)}, f32[16,512]{1,0:T(8,128)S(1)}, u32[]{:S(2)}, u32[]{:S(2)}) collective-permute-start(f32[16,512]{1,0:T(8,128)S(1)} %get-tuple-element.10), channel_id=1, source_target_pairs={{1,0},{2,1},{3,2},{4,3},{5,4},{6,5},{7,6},{8,7},{9,8},{10,9},{11,1... | collective-permute-start | bytes 98312 | tf_op jit(solution)/shard_map/ppermute | solution.py:21
  26.6 0.6 collective-permute-done.2
  27.2 0.2 collective-permute-done.3
  27.4 0.1 reshape.51
  27.5 0.1 copy.41
  27.7 1.0 gather_fusion.1
  28.7 9.3 %fusion.15 = f32[16,32,64]{2,0,1:T(8,128)S(1)} fusion(f32[32,8,64,64]{3,2,1,0:T(8,128)} %param.6, f32[32,8,16,64]{3,2,1,0:T(8,128)S(1)} %bitcast.71, pred[32,8]{1,0:T(8,128)(4,1)S(1)} %copy.35), kind=kOutput, calls=%fused_computation.19 | convolution fusion | flops 201588736 | bytes 5374208 | tf_op jit(solution)/shard_map/irkb,rkab->ira/dot_general | solution.py:56
  38.3 0.3 collective-permute-start.4
  38.6 8.0 %collective-permute-start.5 = (f32[16,512]{1,0:T(8,128)S(1)}, f32[16,512]{1,0:T(8,128)S(1)}, u32[]{:S(2)}, u32[]{:S(2)}) collective-permute-start(f32[16,512]{1,0:T(8,128)S(1)} %get-tuple-element.8), channel_id=1, source_target_pairs={{1,0},{2,1},{3,2},{4,3},{5,4},{6,5},{7,6},{8,7},{9,8},{10,9},{11,1... | collective-permute-start | bytes 98312 | tf_op jit(solution)/shard_map/ppermute | solution.py:21
  46.6 0.6 collective-permute-done.4
  47.2 0.2 collective-permute-done.5
  47.5 0.1 copy.45
  47.7 1.0 gather_fusion.2
  48.7 9.3 %fusion.18 = f32[16,32,64]{2,0,1:T(8,128)S(1)} fusion(f32[32,8,64,64]{3,2,1,0:T(8,128)} %param.6, f32[32,8,16,64]{3,2,1,0:T(8,128)S(1)} %bitcast.72, pred[32,8]{1,0:T(8,128)(4,1)S(1)} %copy.35), kind=kOutput, calls=%fused_computation.20 | convolution fusion | flops 201588736 | bytes 5374208 | tf_op jit(solution)/shard_map/irkb,rkab->ira/dot_general | solution.py:56
  58.4 8.0 %collective-permute-start.7 = (f32[16,512]{1,0:T(8,128)S(1)}, f32[16,512]{1,0:T(8,128)S(1)}, u32[]{:S(2)}, u32[]{:S(2)}) collective-permute-start(f32[16,512]{1,0:T(8,128)S(1)} %get-tuple-element.6), channel_id=1, source_target_pairs={{1,0},{2,1},{3,2},{4,3},{5,4},{6,5},{7,6},{8,7},{9,8},{10,9},{11,1... | collective-permute-start | bytes 98312 | tf_op jit(solution)/shard_map/ppermute | solution.py:21
  66.4 0.6 collective-permute-done.6
  67.0 0.2 collective-permute-done.7
  67.4 0.1 copy.49
  67.5 1.0 gather_fusion.3
  68.5 9.3 %fusion.21 = f32[16,32,64]{2,0,1:T(8,128)S(1)} fusion(f32[32,8,64,64]{3,2,1,0:T(8,128)} %param.6, f32[32,8,16,64]{3,2,1,0:T(8,128)S(1)} %bitcast.69, pred[32,8]{1,0:T(8,128)(4,1)S(1)} %copy.35), kind=kOutput, calls=%fused_computation.21 | convolution fusion | flops 201588736 | bytes 5374208 | tf_op jit(solution)/shard_map/irkb,rkab->ira/dot_general | solution.py:56
  78.1 0.6 fusion.32
  78.7 20.1 %psum.28 = f32[64,64]{0,1:T(8,128)S(1)} all-reduce(f32[64,64]{0,1:T(8,128)S(1)} %fusion.32), channel_id=1, replica_groups=mesh['wide_0'=8,'wide_1'=4,'narrow_0'=4,'narrow_1'=2] {'wide_0'}, use_global_device_ids=true, to_apply=%region_0.2 | all-reduce | flops 4096 | bytes 32768 | tf_op jit(solution)/shard_map/psum | solution.py:34
  98.8 10.9 %psum.29 = f32[64,64]{0,1:T(8,128)S(1)} all-reduce(f32[64,64]{0,1:T(8,128)S(1)} %psum.28), channel_id=1, replica_groups=mesh['wide_0'=8,'wide_1'=4,'narrow_0'=4,'narrow_1'=2] {'wide_1'}, use_global_device_ids=true, to_apply=%region_1.3 | all-reduce | flops 4096 | bytes 32768 | tf_op jit(solution)/shard_map/psum | solution.py:34
  109.7 26.0 %psum.30 = f32[64,64]{0,1:T(8,128)S(1)} all-reduce(f32[64,64]{0,1:T(8,128)S(1)} %psum.29), channel_id=1, replica_groups=mesh['wide_0'=8,'wide_1'=4,'narrow_0'=4,'narrow_1'=2] {'narrow_0'}, use_global_device_ids=true, to_apply=%region_2.4 | all-reduce | flops 4096 | bytes 32768 | tf_op jit(solution)/shard_map/psum | solution.py:34
  135.8 11.2 %psum.31 = f32[64,64]{0,1:T(8,128)S(1)} all-reduce(f32[64,64]{0,1:T(8,128)S(1)} %psum.30), channel_id=1, replica_groups=mesh['wide_0'=8,'wide_1'=4,'narrow_0'=4,'narrow_1'=2] {'narrow_1'}, use_global_device_ids=true, to_apply=%region_3.5 | all-reduce | flops 4096 | bytes 32768 | tf_op jit(solution)/shard_map/psum | solution.py:34
  147.1 5.8 %cholesky.34 = f32[64,64]{1,0:T(8,128)S(1)} custom-call(f32[64,64]{1,0:T(8,128)S(1)} %fusion.46), custom_call_target="Cholesky" | custom-call | tf_op jit(solution)/shard_map/jit(cholesky)/cholesky | solution.py:70
  153.0 0.6 compare_reduce_fusion.1
  153.6 0.7 select_bitcast_fusion
  154.3 0.1 fusion.54
  154.4 0.2 fusion.57
  154.7 4.4 %cholesky.64 = f32[48,48]{1,0:T(8,128)S(1)} custom-call(f32[48,48]{1,0:T(8,128)S(1)} %fusion.53), custom_call_target="Cholesky" | custom-call | tf_op jit(solution)/shard_map/jit(cholesky)/cholesky | solution.py:75
  159.1 0.6 compare_reduce_fusion
  159.8 0.7 fusion.47
  160.4 3.7 %custom-call.11 = f32[1,48,48]{1,2,0:T(8,128)S(1)} custom-call(f32[1,48,48]{2,1,0:T(8,128)S(1)} %fusion.47), custom_call_target="InvertDiagBlocksLowerTriangular" | custom-call | tf_op jit(solution)/shard_map/triangular_solve | solution.py:77
  164.1 0.1 fusion.51
  164.3 0.2 fusion.49
  164.4 1.0 convolution_subtract_fusion
  165.4 1.0 convolution_add_fusion
  (37 shorter events, 1.9 us)
Async XLA Ops:
  1.4 4.3 %collective-permute-start = (f32[16,512]{1,0:T(8,128)S(1)}, f32[16,512]{1,0:T(8,128)S(1)}, u32[]{:S(2)}, u32[]{:S(2)}) collective-permute-start(f32[16,512]{1,0:T(8,128)S(1)} %get-tuple-element.11), channel_id=1, source_target_pairs={{0,1},{1,2},{2,3},{3,4},{4,5},{5,6},{6,7},{7,8},{8,9},{9,10},{10,1... | collective-permute-start | bytes 98312 | tf_op jit(solution)/shard_map/ppermute | solution.py:20
  4.0 3.3 %collective-permute-start.1 = (f32[16,512]{1,0:T(8,128)S(1)}, f32[16,512]{1,0:T(8,128)S(1)}, u32[]{:S(2)}, u32[]{:S(2)}) collective-permute-start(f32[16,512]{1,0:T(8,128)S(1)} %get-tuple-element.12), channel_id=1, source_target_pairs={{1,0},{2,1},{3,2},{4,3},{5,4},{6,5},{7,6},{8,7},{9,8},{10,9},{11,1... | collective-permute-start | bytes 98312 | tf_op jit(solution)/shard_map/ppermute | solution.py:21
  9.6 9.6 %copy-start.1 = (f32[16,2048]{1,0:T(8,128)S(1)}, f32[16,2048]{1,0:T(8,128)}, u32[]{:S(2)}) copy-start(f32[16,2048]{1,0:T(8,128)} %param.8) | copy-start | bytes 393220
  19.2 8.0 %collective-permute-start.2 = (f32[16,512]{1,0:T(8,128)S(1)}, f32[16,512]{1,0:T(8,128)S(1)}, u32[]{:S(2)}, u32[]{:S(2)}) collective-permute-start(f32[16,512]{1,0:T(8,128)S(1)} %get-tuple-element.9), channel_id=1, source_target_pairs={{0,1},{1,2},{2,3},{3,4},{4,5},{5,6},{6,7},{7,8},{8,9},{9,10},{10,1... | collective-permute-start | bytes 98312 | tf_op jit(solution)/shard_map/ppermute | solution.py:20
  19.3 8.1 %collective-permute-start.3 = (f32[16,512]{1,0:T(8,128)S(1)}, f32[16,512]{1,0:T(8,128)S(1)}, u32[]{:S(2)}, u32[]{:S(2)}) collective-permute-start(f32[16,512]{1,0:T(8,128)S(1)} %get-tuple-element.10), channel_id=1, source_target_pairs={{1,0},{2,1},{3,2},{4,3},{5,4},{6,5},{7,6},{8,7},{9,8},{10,9},{11,1... | collective-permute-start | bytes 98312 | tf_op jit(solution)/shard_map/ppermute | solution.py:21
  38.3 8.9 %collective-permute-start.4 = (f32[16,512]{1,0:T(8,128)S(1)}, f32[16,512]{1,0:T(8,128)S(1)}, u32[]{:S(2)}, u32[]{:S(2)}) collective-permute-start(f32[16,512]{1,0:T(8,128)S(1)} %get-tuple-element.7), channel_id=1, source_target_pairs={{0,1},{1,2},{2,3},{3,4},{4,5},{5,6},{6,7},{7,8},{8,9},{9,10},{10,1... | collective-permute-start | bytes 98312 | tf_op jit(solution)/shard_map/ppermute | solution.py:20
  38.6 8.8 %collective-permute-start.5 = (f32[16,512]{1,0:T(8,128)S(1)}, f32[16,512]{1,0:T(8,128)S(1)}, u32[]{:S(2)}, u32[]{:S(2)}) collective-permute-start(f32[16,512]{1,0:T(8,128)S(1)} %get-tuple-element.8), channel_id=1, source_target_pairs={{1,0},{2,1},{3,2},{4,3},{5,4},{6,5},{7,6},{8,7},{9,8},{10,9},{11,1... | collective-permute-start | bytes 98312 | tf_op jit(solution)/shard_map/ppermute | solution.py:21
  58.3 8.7 %collective-permute-start.6 = (f32[16,512]{1,0:T(8,128)S(1)}, f32[16,512]{1,0:T(8,128)S(1)}, u32[]{:S(2)}, u32[]{:S(2)}) collective-permute-start(f32[16,512]{1,0:T(8,128)S(1)} %get-tuple-element.5), channel_id=1, source_target_pairs={{0,1},{1,2},{2,3},{3,4},{4,5},{5,6},{6,7},{7,8},{8,9},{9,10},{10,1... | collective-permute-start | bytes 98312 | tf_op jit(solution)/shard_map/ppermute | solution.py:20
  58.4 8.8 %collective-permute-start.7 = (f32[16,512]{1,0:T(8,128)S(1)}, f32[16,512]{1,0:T(8,128)S(1)}, u32[]{:S(2)}, u32[]{:S(2)}) collective-permute-start(f32[16,512]{1,0:T(8,128)S(1)} %get-tuple-element.6), channel_id=1, source_target_pairs={{1,0},{2,1},{3,2},{4,3},{5,4},{6,5},{7,6},{8,7},{9,8},{10,9},{11,1... | collective-permute-start | bytes 98312 | tf_op jit(solution)/shard_map/ppermute | solution.py:21
  78.0 87.5 %copy-start = (f32[16,2048]{1,0:T(8,128)S(1)}, f32[16,2048]{1,0:T(8,128)}, u32[]{:S(2)}) copy-start(f32[16,2048]{1,0:T(8,128)} %param.9) | copy-start | bytes 393220
where the time goes:
time: 167 us; the launch traced here: 166 us
  blocking collectives  68.3 us (41%)
  matrix products  40.5 us (24%)
  starting transfers between devices  27 us (16%)
  other arithmetic  18.3 us (11%)
  local copies, waits for them, and re-layouts  7.13 us (4%)
  waiting for transfers between devices  4.22 us (3%)
    psum x4, blocking collectives, one_axis_at_a_time(): array = lax.psum(array, axis)  68.3 us
    dot_general x4, matrix products, apply_matrix(): jnp.einsum('irkb,rkab->ira', picked, blocks, precision=lax.Precision.HIGH...  37.3 us
    ppermute x4, starting transfers between devices, with_halo(): lax.ppermute(first, axis, [(b, a) for a, b in up])  24 us
    another operation x3, other arithmetic, per_device(): upper = jnp.linalg.cholesky(gram).T  6.52 us
    another operation x3, other arithmetic, per_device(): factor = jnp.linalg.cholesky(normal)  5.05 us
    another operation x2, other arithmetic, per_device(): lax.linalg.triangular_solve(factor, middle, left_side=True, lower=True, t...  4.32 us
    gather x4, local copies, waits for them, and re-layouts, apply_matrix(): picked = jnp.take(shaped, position, axis=1)  4.07 us
  transfers between devices with their start and end apart: 8, of which 7 were waited for; matrix products, arithmetic and copies ran while one was open for 1% of the time, Pallas kernels for 0%

commit v1 on v0

v1 whole, which is shorter than its diff:
```python
import functools

import jax
import jax.numpy as jnp
from jax import lax
from jax.experimental import pallas as pl
from jax.experimental.pallas import tpu as pltpu
from jax.sharding import Mesh
from jax.sharding import PartitionSpec as P

BS = 64
NNZB = 8
NRHS = 16
S = 4
BAND = 8
ROWS = 32
PAIRS = ROWS // 2
EDGE = BAND // 2
CHUNK = 4
AXES = ("z", "y", "x", "c")
F32 = jnp.float32
BF16 = jnp.bfloat16


def split(v):
    high = v.astype(BF16)
    low = (v - high.astype(F32)).astype(BF16)
    return high, low


def dot_nt(a, b):
    return lax.dot_general(a, b, (((1,), (1,)), ((), ())), preferred_element_type=F32)


def kernel(sizes, col_ref, blocks_hbm, b_hbm, x_hbm, guess_hbm, resid_hbm,
           at_ref, raw, mat, b_ref, x_ref, vec, dup, basis, halves, halo, gram_out, gram_in,
           guess, resid, raw_sem, in_sem, halo0_send, halo0_recv, halo_send, halo_recv,
           red_send, red_recv, out_sem):
    nz, ny, nx, nc = sizes
    total = nz * ny * nx * nc
    here = tuple(lax.axis_index(a) for a in AXES)
    z, y, x, c = here
    linear = ((z * ny + y) * nx + x) * nc + c

    def place(d):
        return (d // (ny * nx * nc), (d // (nx * nc)) % ny, (d // nc) % nx, d % nc)

    up = place((linear + 1) % total)
    down = place((linear + total - 1) % total)

    def narrow_peer(o):
        d = (x * nc + c + o) % (nx * nc)
        return (z, y, d // nc, d % nc)

    def y_peer(o):
        return (z, (y + o) % ny, x, c)

    def z_peer(o):
        return ((z + o) % nz, y, x, c)

    phases = ((nx * nc, narrow_peer), (ny, y_peer), (nz, z_peer))

    def to_remote(src, dst, send, recv, dev):
        return pltpu.make_async_remote_copy(
            src_ref=src, dst_ref=dst, send_sem=send, recv_sem=recv,
            device_id=dev, device_id_type=pl.DeviceIdType.MESH)

    barrier = pltpu.get_barrier_semaphore()
    count = 2
    for dev in (up, down):
        pl.semaphore_signal(barrier, inc=1, device_id=dev, device_id_type=pl.DeviceIdType.MESH)
    for n, peer in phases:
        for o in range(1, n):
            count += 1
            pl.semaphore_signal(barrier, inc=1, device_id=peer(o),
                                device_id_type=pl.DeviceIdType.MESH)

    load_x = pltpu.make_async_copy(x_hbm, x_ref, in_sem.at[0])
    load_b = pltpu.make_async_copy(b_hbm, b_ref, in_sem.at[1])
    load_x.start()
    load_b.start()

    def load_blocks(n):
        rows = pl.ds(n * CHUNK, CHUNK)
        return pltpu.make_async_copy(blocks_hbm.at[rows], raw.at[rows], raw_sem.at[n])

    for n in range(ROWS // CHUNK):
        load_blocks(n).start()
    first_row = linear * ROWS

    def locate(g, _):
        for k in range(NNZB):
            at = jnp.bitwise_and(col_ref[k, g] - first_row + BAND + total * ROWS,
                                 total * ROWS - 1)
            at_ref[k, g] = jnp.minimum(at, ROWS + 2 * BAND - 1)
        return 0

    lax.fori_loop(0, ROWS, locate, 0)
    pl.semaphore_wait(barrier, count)

    def first_halo(side, q):
        tile = q if side == 1 else PAIRS - EDGE + q
        return to_remote(x_hbm.at[:, pl.ds(tile * 128, 128)], halo.at[0, side, q],
                         halo0_send.at[side, q], halo0_recv.at[side, q],
                         down if side == 1 else up)

    def later_halo(j, side):
        start = 0 if side == 1 else PAIRS - EDGE
        return to_remote(basis.at[j - 1, pl.ds(start, EDGE)], halo.at[j, side],
                         halo_send.at[j - 1, side], halo_recv.at[j - 1, side],
                         down if side == 1 else up)

    for q in range(EDGE):
        for side in range(2):
            first_halo(side, q).start()

    left = lax.broadcasted_iota(jnp.int32, (NRHS, 128), 1) < BS
    left2 = lax.broadcasted_iota(jnp.int32, (2 * NRHS, 128), 1) < BS

    def both(v):
        r = pltpu.roll(v, BS, 1)
        return jnp.where(left, v, r), jnp.where(left, r, v)

    def put(j, row, v):
        high, low = split(v)
        vec[j, row, 0:NRHS] = high
        vec[j, row, NRHS:2 * NRHS] = low

    load_x.wait()
    load_b.wait()

    def spread(p, _):
        lanes = pl.ds(pl.multiple_of(p * 128, 128), 128)
        v0, v1 = both(-x_ref[:, lanes])
        put(0, BAND + 2 * p, v0)
        put(0, BAND + 2 * p + 1, v1)
        w0, w1 = both(b_ref[:, lanes])
        dup[2 * p] = w0
        dup[2 * p + 1] = w1
        return 0

    lax.fori_loop(0, PAIRS, spread, 0)

    def prepare_row(g):
        for m in range(NNZB // 2):
            wide = jnp.concatenate([raw[g, 2 * m], raw[g, 2 * m + 1]], axis=1)
            high, low = split(wide)
            mat[g, 0:BS, m * 128:(m + 1) * 128] = high
            mat[g, BS:2 * BS, m * 128:(m + 1) * 128] = low

    def prepare(n, _):
        load_blocks(n).wait()
        for r in range(CHUNK):
            prepare_row(n * CHUNK + r)
        return 0

    lax.fori_loop(0, ROWS // CHUNK, prepare, 0)

    def apply_row(j, g, beta):
        tiles = []
        for m in range(NNZB // 2):
            part = []
            for k in (2 * m, 2 * m + 1):
                part.append(vec[j, at_ref[k, g]])
            tiles.append(jnp.where(left2, part[0], part[1]))
        out = dot_nt(jnp.concatenate(tiles, axis=1), mat[g])
        half = out[0:NRHS] + out[NRHS:2 * NRHS]
        v = half + pltpu.roll(half, BS, 1) + beta * dup[g]
        dup[g] = v
        put(j + 1, BAND + g, v)
        return v

    def apply_pair(j, p, beta):
        v0 = apply_row(j, 2 * p, beta)
        v1 = apply_row(j, 2 * p + 1, beta)
        v = jnp.where(left, v0, v1)
        basis[j, p] = v
        high, low = split(v)
        halves[p, 0, j] = high
        halves[p, 1, j] = low

    def apply_pairs(j, start, n, beta):
        def body(i, _):
            for t in range(4):
                apply_pair(j, start + i * 4 + t, beta)
            return 0
        lax.fori_loop(0, n // 4, body, 0)

    def take_halo(j, side, sign):
        for q in range(EDGE):
            v0, v1 = both(sign * halo[j, side, q])
            row = 2 * q + (0 if side == 0 else BAND + ROWS)
            put(j, row, v0)
            put(j, row + 1, v1)

    def step(j, _):
        beta = jnp.where(j == 0, 1.0, -2.0)
        sign = jnp.where(j == 0, -1.0, 1.0)
        apply_pairs(j, EDGE, PAIRS - 2 * EDGE, beta)

        @pl.when(j == 0)
        def _():
            for side in range(2):
                for q in range(EDGE):
                    first_halo(side, q).wait_recv()

        @pl.when(j > 0)
        def _():
            for side in range(2):
                later_halo(j, side).wait_recv()

        take_halo(j, 0, sign)
        take_halo(j, 1, sign)
        for side in (1, 0):
            start = 0 if side == 1 else PAIRS - EDGE
            apply_pairs(j, start, EDGE, beta)

            @pl.when(j < S - 1)
            def _():
                later_halo(j + 1, side).start()
        return 0

    lax.fori_loop(0, S, step, 0)

    gram = jnp.zeros((2 * S * NRHS, 128), F32)
    for p in range(0, PAIRS, 2):
        tile = jnp.concatenate([halves[p].reshape(2 * S * NRHS, 128),
                                halves[p + 1].reshape(2 * S * NRHS, 128)], axis=1)
        gram = gram + dot_nt(tile, tile)
    gram = gram[0:64] + gram[64:128]
    gram = gram + pltpu.roll(gram, 64, 1)
    left3 = lax.broadcasted_iota(jnp.int32, (32, 128), 1) < 64
    packed = jnp.where(left3, gram[0:32], gram[32:64])

    sent = []
    base = 0
    for f, (n, peer) in enumerate(phases):
        gram_out[f] = packed
        copies = []
        for o in range(1, n):
            copy = to_remote(gram_out.at[f], gram_in.at[base + o - 1],
                             red_send.at[base + o - 1], red_recv.at[base + o - 1], peer(o))
            copy.start()
            copies.append(copy)
        for o in range(1, n):
            copies[o - 1].wait_recv()
            packed = packed + gram_in[base + o - 1]
        sent += copies
        base += n - 1

    turned = pltpu.roll(packed, 64, 1)
    gram = jnp.concatenate([jnp.where(left3, packed, turned),
                            jnp.where(left3, turned, packed)], axis=0)

    lane = lax.broadcasted_iota(jnp.int32, (48, 128), 1)
    sub = lax.broadcasted_iota(jnp.int32, (48, 128), 0)
    hess = gram[16:64] + 2.0 * gram[0:48]
    system = pltpu.roll(hess, 112, 1) + jnp.where(lane % 64 < 48, 2.0 * hess, 0.0)
    for k in range(48):
        row = jnp.broadcast_to(system[k:k + 1, :], (48, 128))
        col = jnp.broadcast_to(system[:, k:k + 1], (48, 128))
        scaled = row * (1.0 / jnp.broadcast_to(system[k:k + 1, k:k + 1], (1, 128)))
        system = jnp.where(sub == k, scaled, system - col * scaled)

    none = jnp.zeros((16, 128), F32)
    low_coeff = jnp.concatenate([system, none], axis=0)
    high_coeff = jnp.concatenate([none, system], axis=0) + 2.0 * low_coeff
    lane = lax.broadcasted_iota(jnp.int32, (64, 128), 1)
    mix = jnp.where(lane < 16, pltpu.roll(low_coeff, 80, 1), pltpu.roll(-high_coeff, 96, 1))
    mix = jnp.transpose(mix)[0:32]

    outs = []
    for p in range(0, PAIRS, 4):
        tile = jnp.concatenate([basis[:, p + t].reshape(64, 128) for t in range(4)], axis=1)
        out = jnp.dot(mix, tile, precision=lax.Precision.HIGHEST, preferred_element_type=F32)
        lanes = slice(p * 128, (p + 4) * 128)
        guess[:, lanes] = x_ref[:, lanes] + out[0:16]
        resid[:, lanes] = tile[0:16] + out[16:32]
        for w, (src, dst) in enumerate(((guess, guess_hbm), (resid, resid_hbm))):
            copy = pltpu.make_async_copy(src.at[:, lanes], dst.at[:, lanes],
                                         out_sem.at[w, p // 4])
            copy.start()
            outs.append(copy)

    for side in range(2):
        for q in range(EDGE):
            first_halo(side, q).wait_send()
        for j in range(1, S):
            later_halo(j, side).wait_send()
    for copy in sent:
        copy.wait_send()
    for copy in outs:
        copy.wait()


def per_device(sizes, blocks, col_index, right_side, start_guess):
    n_red = sizes[0] - 1 + sizes[1] - 1 + sizes[2] * sizes[3] - 1
    anywhere = pl.BlockSpec(memory_space=pltpu.HBM)
    dma = pltpu.SemaphoreType.DMA
    out = jax.ShapeDtypeStruct((NRHS, ROWS * BS), F32)
    return pl.pallas_call(
        functools.partial(kernel, sizes),
        out_shape=(out, out),
        in_specs=[pl.BlockSpec(memory_space=pltpu.SMEM), anywhere, anywhere, anywhere],
        out_specs=(anywhere, anywhere),
        scratch_shapes=[
            pltpu.SMEM((NNZB, ROWS), jnp.int32),
            pltpu.VMEM((ROWS, NNZB, BS, BS), F32),
            pltpu.VMEM((ROWS, 2 * BS, NNZB * BS), BF16),
            pltpu.VMEM((NRHS, ROWS * BS), F32),
            pltpu.VMEM((NRHS, ROWS * BS), F32),
            pltpu.VMEM((S + 1, ROWS + 2 * BAND, 2 * NRHS, 128), BF16),
            pltpu.VMEM((ROWS, NRHS, 128), F32),
            pltpu.VMEM((S, PAIRS, NRHS, 128), F32),
            pltpu.VMEM((PAIRS, 2, S, NRHS, 128), BF16),
            pltpu.VMEM((S, 2, EDGE, NRHS, 128), F32),
            pltpu.VMEM((3, 32, 128), F32),
            pltpu.VMEM((n_red, 32, 128), F32),
            pltpu.VMEM((NRHS, ROWS * BS), F32),
            pltpu.VMEM((NRHS, ROWS * BS), F32),
            dma((ROWS // CHUNK,)),
            dma((2,)),
            dma((2, EDGE)),
            dma((2, EDGE)),
            dma((S - 1, 2)),
            dma((S - 1, 2)),
            dma((n_red,)),
            dma((n_red,)),
            dma((2, PAIRS // 4)),
        ],
        compiler_params=pltpu.CompilerParams(
            collective_id=0, has_side_effects=True, vmem_limit_bytes=48 * 1024 * 1024),
        name="gmres_cycle",
    )(col_index.T, blocks, right_side, start_guess)


def solution(mesh, sizes=(8, 4, 4, 2)):
    torus = Mesh(mesh.devices.reshape(sizes), AXES)
    in_specs = (P(AXES, None, None, None), P(AXES, None), P(None, AXES), P(None, AXES))
    out_specs = (P(None, AXES), P(None, AXES))
    return jax.shard_map(functools.partial(per_device, sizes), mesh=torus, in_specs=in_specs,
                         out_specs=out_specs, check_vma=False)
```

time: 167 us -> 67.5 us (0.40)
  blocking collectives: 68.3 us -> 0 us
  Pallas kernels: 0 us -> 62.3 us
  matrix products: 40.5 us -> 0 us
  starting transfers between devices: 27 us -> 0 us
  other arithmetic: 18.3 us -> 0 us
  waiting for transfers between devices: 4.22 us -> 0 us
  local copies, waits for them, and re-layouts: 7.13 us -> 3.8 us
    psum x4 -> x0, blocking collectives: 68.3 us -> none  [one_axis_at_a_time(): array = lax.psum(array, axis)]
    pallas_call x0 -> x1, Pallas kernels: none -> 62.3 us  [per_device(): pl.pallas_call(functools.partial(kernel, sizes), out_shape=(out, out), in...]
    dot_general x9 -> x0, matrix products: 40.2 us -> none  [the longest x4 37.3 us: apply_matrix(): jnp.einsum('irkb,rkab->ira', picked, blocks, precision=lax.Precision.HIGH...]
    ppermute x8 -> x0, starting transfers between devices: 27 us -> none  [the longest x4 24 us: with_halo(): lax.ppermute(first, axis, [(b, a) for a, b in up])]
    another operation x8 -> x0, other arithmetic: 15.9 us -> none  [the longest x3 6.52 us: per_device(): upper = jnp.linalg.cholesky(gram).T]
    ppermute x8 -> x0, waiting for transfers between devices: 4.22 us -> none  [the longest x4 2.38 us: with_halo(): lax.ppermute(first, axis, [(b, a) for a, b in up])]
    gather x4 -> x0, local copies, waits for them, and re-layouts: 4.07 us -> none  [apply_matrix(): picked = jnp.take(shaped, position, axis=1)]
    unnamed x4 -> x8, local copies, waits for them, and re-layouts: 0.01 us -> 3.8 us
  transfers between devices with their start and end apart: 8 -> 0, of which waited for: 7 -> 0; matrix products, arithmetic and copies ran while one was open for 1% -> 0% of each run, Pallas kernels for 0% -> 0%
where the time goes in v1:
time: 67.5 us; the launch traced here: 66.8 us
  Pallas kernels  62.3 us (92%)
  local copies, waits for them, and re-layouts  3.8 us (6%)
    pallas_call x1, Pallas kernels, per_device(): pl.pallas_call(functools.partial(kernel, sizes), out_shape=(out, out), in...  62.3 us
    unnamed x8, local copies, waits for them, and re-layouts  3.8 us

profile of v1, /device:TPU:1, one launch (start us, length us, event | category | flops | bytes accessed | tf_op | source)
XLA Modules:
  0.0 66.8 jit_solution(2592961331686542595)
XLA Ops:
  0.6 0.0 copy-start
  0.6 0.9 %copy-done = f32[16,2048]{1,0:T(8,128)S(1)} copy-done((f32[16,2048]{1,0:T(8,128)S(1)}, f32[16,2048]{1,0:T(8,128)}, u32[]{:S(2)}) %copy-start) | copy-done | bytes 131096
  1.5 0.0 copy-start.1
  1.5 0.9 %copy-done.1 = f32[16,2048]{1,0:T(8,128)S(1)} copy-done((f32[16,2048]{1,0:T(8,128)S(1)}, f32[16,2048]{1,0:T(8,128)}, u32[]{:S(2)}) %copy-start.1) | copy-done | bytes 131096
  2.4 0.0 copy-start.2
  2.4 0.7 %copy-done.2 = s32[32,8]{0,1:T(8,128)S(1)} copy-done((s32[32,8]{0,1:T(8,128)S(1)}, s32[32,8]{0,1:T(8,128)}, u32[]{:S(2)}) %copy-start.2) | copy-done | bytes 1048
  3.1 62.3 %gmres_cycle.1 = (f32[16,2048]{1,0:T(8,128)S(1)}, f32[16,2048]{1,0:T(8,128)S(1)}) custom-call(s32[8,32]{1,0:T(8,128)S(1)} %bitcast.1, f32[32,8,64,64]{3,2,1,0:T(8,128)} %blocks_hbm.1, f32[16,2048]{1,0:T(8,128)S(1)} %copy-done, f32[16,2048]{1,0:T(8,128)S(1)} %copy-done.1), custom_call_target="tpu_custom_call" | custom-call | tf_op jit(solution)/shard_map/gmres_cycle/pallas_call | solution.py:301
  65.5 0.7 copy.8
  66.1 0.7 copy.9
Async XLA Ops:
  0.6 0.9 %copy-start = (f32[16,2048]{1,0:T(8,128)S(1)}, f32[16,2048]{1,0:T(8,128)}, u32[]{:S(2)}) copy-start(f32[16,2048]{1,0:T(8,128)} %b_hbm.1) | copy-start | bytes 393220
  1.5 0.9 %copy-start.1 = (f32[16,2048]{1,0:T(8,128)S(1)}, f32[16,2048]{1,0:T(8,128)}, u32[]{:S(2)}) copy-start(f32[16,2048]{1,0:T(8,128)} %x_hbm.1) | copy-start | bytes 393220
  2.4 0.7 %copy-start.2 = (s32[32,8]{0,1:T(8,128)S(1)}, s32[32,8]{0,1:T(8,128)}, u32[]{:S(2)}) copy-start(s32[32,8]{0,1:T(8,128)} %param.5) | copy-start | bytes 3076

commit v2 on v1

--- a/solution.py
+++ b/solution.py
@@ -32,8 +32,19 @@
     return lax.dot_general(a, b, (((1,), (1,)), ((), ())), preferred_element_type=F32)
 
 
+def eliminate(system, start, n):
+    rows = system.shape[0]
+    sub = lax.broadcasted_iota(jnp.int32, system.shape, 0)
+    for k in range(start, start + n):
+        row = jnp.broadcast_to(system[k:k + 1, :], system.shape)
+        col = jnp.broadcast_to(system[:, k:k + 1], system.shape)
+        scaled = row * (1.0 / jnp.broadcast_to(system[k:k + 1, k:k + 1], (1, 128)))
+        system = jnp.where(sub == k, scaled, system - col * scaled)
+    return system
+
+
 def kernel(sizes, col_ref, blocks_hbm, b_hbm, x_hbm, guess_hbm, resid_hbm,
-           at_ref, raw, mat, b_ref, x_ref, vec, dup, basis, halves, halo, gram_out, gram_in,
+           at_ref, raw, mat, b_ref, x_ref, vec, dup, basis, halves, halo, early_out, early_in, late_out, late_in,
            guess, resid, raw_sem, in_sem, halo0_send, halo0_recv, halo_send, halo_recv,
            red_send, red_recv, out_sem):
     nz, ny, nx, nc = sizes
@@ -48,17 +59,14 @@
     up = place((linear + 1) % total)
     down = place((linear + total - 1) % total)
 
-    def narrow_peer(o):
-        d = (x * nc + c + o) % (nx * nc)
-        return (z, y, d // nc, d % nc)
-
-    def y_peer(o):
-        return (z, (y + o) % ny, x, c)
+    def plane_peer(o):
+        d = ((y * nx + x) * nc + c + o) % (ny * nx * nc)
+        return (z, d // (nx * nc), (d // nc) % nx, d % nc)
 
     def z_peer(o):
         return ((z + o) % nz, y, x, c)
 
-    phases = ((nx * nc, narrow_peer), (ny, y_peer), (nz, z_peer))
+    phases = ((ny * nx * nc, plane_peer), (nz, z_peer))
 
     def to_remote(src, dst, send, recv, dev):
         return pltpu.make_async_remote_copy(
@@ -156,35 +164,29 @@
 
     lax.fori_loop(0, ROWS // CHUNK, prepare, 0)
 
-    def apply_row(j, g, beta):
-        tiles = []
-        for m in range(NNZB // 2):
-            part = []
-            for k in (2 * m, 2 * m + 1):
-                part.append(vec[j, at_ref[k, g]])
-            tiles.append(jnp.where(left2, part[0], part[1]))
-        out = dot_nt(jnp.concatenate(tiles, axis=1), mat[g])
-        half = out[0:NRHS] + out[NRHS:2 * NRHS]
-        v = half + pltpu.roll(half, BS, 1) + beta * dup[g]
-        dup[g] = v
-        put(j + 1, BAND + g, v)
-        return v
-
-    def apply_pair(j, p, beta):
-        v0 = apply_row(j, 2 * p, beta)
-        v1 = apply_row(j, 2 * p + 1, beta)
-        v = jnp.where(left, v0, v1)
-        basis[j, p] = v
-        high, low = split(v)
-        halves[p, 0, j] = high
-        halves[p, 1, j] = low
-
-    def apply_pairs(j, start, n, beta):
-        def body(i, _):
-            for t in range(4):
-                apply_pair(j, start + i * 4 + t, beta)
-            return 0
-        lax.fori_loop(0, n // 4, body, 0)
+    def apply_pairs(j, pairs, beta):
+        halfs = []
+        for p in pairs:
+            for g in (2 * p, 2 * p + 1):
+                tiles = []
+                for m in range(NNZB // 2):
+                    tiles.append(jnp.where(left2, vec[j, at_ref[2 * m, g]],
+                                           vec[j, at_ref[2 * m + 1, g]]))
+                out = dot_nt(jnp.concatenate(tiles, axis=1), mat[g])
+                halfs.append(out[0:NRHS] + out[NRHS:2 * NRHS])
+        for i, p in enumerate(pairs):
+            v = []
+            for g in (0, 1):
+                half = halfs[2 * i + g]
+                v.append(half + pltpu.roll(half, BS, 1) + beta * dup[2 * p + g])
+            for g in (0, 1):
+                dup[2 * p + g] = v[g]
+                put(j + 1, BAND + 2 * p + g, v[g])
+            both_rows = jnp.where(left, v[0], v[1])
+            basis[j, p] = both_rows
+            high, low = split(both_rows)
+            halves[p, 0, j] = high
+            halves[p, 1, j] = low
 
     def take_halo(j, side, sign):
         for q in range(EDGE):
@@ -193,74 +195,138 @@
             put(j, row, v0)
             put(j, row + 1, v1)
 
-    def step(j, _):
-        beta = jnp.where(j == 0, 1.0, -2.0)
-        sign = jnp.where(j == 0, -1.0, 1.0)
-        apply_pairs(j, EDGE, PAIRS - 2 * EDGE, beta)
-
-        @pl.when(j == 0)
-        def _():
-            for side in range(2):
-                for q in range(EDGE):
-                    first_halo(side, q).wait_recv()
-
-        @pl.when(j > 0)
-        def _():
-            for side in range(2):
-                later_halo(j, side).wait_recv()
-
+    def wait_first():
+        for side in range(2):
+            for q in range(EDGE):
+                first_halo(side, q).wait_recv()
+
+    def wait_later(j):
+        for side in range(2):
+            later_halo(j, side).wait_recv()
+
+    def edges(j, beta, sign, last):
         take_halo(j, 0, sign)
         take_halo(j, 1, sign)
         for side in (1, 0):
             start = 0 if side == 1 else PAIRS - EDGE
-            apply_pairs(j, start, EDGE, beta)
-
-            @pl.when(j < S - 1)
-            def _():
+            apply_pairs(j, range(start, start + EDGE), beta)
+            if not last:
                 later_halo(j + 1, side).start()
+
+    def step(j, _):
+        beta = jnp.where(j == 0, 1.0, -2.0)
+        sign = jnp.where(j == 0, -1.0, 1.0)
+        apply_pairs(j, range(EDGE, PAIRS - EDGE), beta)
+
+        @pl.when(j == 0)
+        def _():
+            wait_first()
+
+        @pl.when(j > 0)
+        def _():
+            wait_later(j)
+
+        edges(j, beta, sign, False)
         return 0
 
-    lax.fori_loop(0, S, step, 0)
-
-    gram = jnp.zeros((2 * S * NRHS, 128), F32)
-    for p in range(0, PAIRS, 2):
-        tile = jnp.concatenate([halves[p].reshape(2 * S * NRHS, 128),
-                                halves[p + 1].reshape(2 * S * NRHS, 128)], axis=1)
-        gram = gram + dot_nt(tile, tile)
-    gram = gram[0:64] + gram[64:128]
-    gram = gram + pltpu.roll(gram, 64, 1)
-    left3 = lax.broadcasted_iota(jnp.int32, (32, 128), 1) < 64
-    packed = jnp.where(left3, gram[0:32], gram[32:64])
-
-    sent = []
+    def products(rows, cols, start, n):
+        total_products = None
+        for p in range(start, start + n, 2):
+            def tile(js):
+                return jnp.concatenate(
+                    [halves[q][:, js].reshape(2 * len(range(S)[js]) * NRHS, 128)
+                     for q in (p, p + 1)], axis=1)
+            part = dot_nt(tile(rows), tile(cols))
+            total_products = part if total_products is None else total_products + part
+        return total_products
+
+    def fold(g):
+        n = g.shape[0] // 2
+        g = g[0:n] + g[n:2 * n]
+        return g + pltpu.roll(g, 64, 1)
+
+    def pack(g):
+        n = g.shape[0] // 2
+        mask = lax.broadcasted_iota(jnp.int32, (n, 128), 1) < 64
+        return jnp.where(mask, g[0:n], g[n:2 * n])
+
+    def unpack(g):
+        n = g.shape[0]
+        mask = lax.broadcasted_iota(jnp.int32, (n, 128), 1) < 64
+        r = pltpu.roll(g, 64, 1)
+        return jnp.concatenate([jnp.where(mask, g, r), jnp.where(mask, r, g)], axis=0)
+
+    spans = []
     base = 0
-    for f, (n, peer) in enumerate(phases):
-        gram_out[f] = packed
-        copies = []
-        for o in range(1, n):
-            copy = to_remote(gram_out.at[f], gram_in.at[base + o - 1],
-                             red_send.at[base + o - 1], red_recv.at[base + o - 1], peer(o))
+    for n, _ in phases:
+        spans.append((base, n))
+        base += n - 1
+
+    def sum_copies(r, f):
+        out, inn = (early_out, early_in) if r == 0 else (late_out, late_in)
+        base, n = spans[f]
+        return [to_remote(out.at[f], inn.at[base + o - 1], red_send.at[r, base + o - 1],
+                          red_recv.at[r, base + o - 1], phases[f][1](o)) for o in range(1, n)]
+
+    def sum_start(r, f, value):
+        (early_out if r == 0 else late_out)[f] = value
+        for copy in sum_copies(r, f):
             copy.start()
-            copies.append(copy)
-        for o in range(1, n):
-            copies[o - 1].wait_recv()
-            packed = packed + gram_in[base + o - 1]
-        sent += copies
-        base += n - 1
-
-    turned = pltpu.roll(packed, 64, 1)
-    gram = jnp.concatenate([jnp.where(left3, packed, turned),
-                            jnp.where(left3, turned, packed)], axis=0)
-
-    lane = lax.broadcasted_iota(jnp.int32, (48, 128), 1)
-    sub = lax.broadcasted_iota(jnp.int32, (48, 128), 0)
-    hess = gram[16:64] + 2.0 * gram[0:48]
-    system = pltpu.roll(hess, 112, 1) + jnp.where(lane % 64 < 48, 2.0 * hess, 0.0)
-    for k in range(48):
-        row = jnp.broadcast_to(system[k:k + 1, :], (48, 128))
-        col = jnp.broadcast_to(system[:, k:k + 1], (48, 128))
-        scaled = row * (1.0 / jnp.broadcast_to(system[k:k + 1, k:k + 1], (1, 128)))
-        system = jnp.where(sub == k, scaled, system - col * scaled)
+
+    def sum_finish(r, f, value):
+        inn = early_in if r == 0 else late_in
+        base, n = spans[f]
+        for o, copy in enumerate(sum_copies(r, f)):
+            copy.wait_recv()
+        parts = [value] + [inn[base + o] for o in range(n - 1)]
+        while len(parts) > 1:
+            parts = [parts[i] + parts[i + 1] if i + 1 < len(parts) else parts[i]
+                     for i in range(0, len(parts), 2)]
+        return parts[0]
+
+    lax.fori_loop(0, S - 1, step, 0)
+    halves[:, :, S - 1] = jnp.zeros((PAIRS, 2, NRHS, 128), BF16)
+    gram = products(slice(0, 3), slice(0, 4), 0, PAIRS)
+    early = pack(fold(gram))
+    sum_start(0, 0, early)
+    apply_pairs(S - 1, range(EDGE, PAIRS - EDGE), -2.0)
+    wait_later(S - 1)
+    edges(S - 1, -2.0, 1.0, True)
+    late = pack(fold(products(slice(3, 4), slice(0, 4), 0, PAIRS)))
+    sum_start(1, 0, late)
+    early = sum_finish(0, 0, early)
+    sum_start(0, 1, early)
+    late = sum_finish(1, 0, late)
+    sum_start(1, 1, late)
+    early = sum_finish(0, 1, early)
+
+    gram = unpack(early)
+    lane32 = lax.broadcasted_iota(jnp.int32, (32, 128), 1)
+    sub32 = lax.broadcasted_iota(jnp.int32, (32, 128), 0)
+    hess = gram[16:48] + 2.0 * gram[0:32]
+    system = pltpu.roll(hess, 112, 1) + jnp.where(lane32 % 64 < 48, 2.0 * hess, 0.0)
+    system = jnp.where(lane32 < 64, system, jnp.where(lane32 - 64 == sub32, 1.0, 0.0))
+    system = eliminate(system, 0, 32)
+
+    late = unpack(sum_finish(1, 1, late))
+    lane16 = lax.broadcasted_iota(jnp.int32, (16, 128), 1)
+    turned = jnp.transpose(jnp.concatenate([late, jnp.zeros((112, 128), F32)], axis=0))
+    row2 = jnp.where(lane16 % 64 < 48, gram[32:48],
+                     pltpu.roll(turned[32:48], 48, 1))
+    hess2 = late + 2.0 * row2
+    cross = pltpu.roll(hess2, 112, 1) + jnp.where(lane16 % 64 < 48, 2.0 * hess2, 0.0)
+    hp = lax.Precision.HIGHEST
+    moved = jnp.dot(cross[:, 0:32], system, precision=hp, preferred_element_type=F32)
+    inner = lax.dot_general(moved[:, 64:96], cross[:, 0:32], (((1,), (1,)), ((), ())),
+                            precision=hp, preferred_element_type=F32)
+    inner = jnp.concatenate([inner, jnp.zeros((16, 112), F32)], axis=1)
+    schur = jnp.where(lane16 < 16, pltpu.roll(cross, 96, 1) - inner,
+                      pltpu.roll(cross - moved, 96, 1))
+    schur = eliminate(schur, 0, 16)
+    last = pltpu.roll(schur, 32, 1)
+    back = jnp.transpose(jnp.concatenate([moved, jnp.zeros((112, 128), F32)], axis=0))[64:96, 0:16]
+    first = system - jnp.dot(back, last, precision=hp, preferred_element_type=F32)
+    system = jnp.concatenate([first, last], axis=0)
 
     none = jnp.zeros((16, 128), F32)
     low_coeff = jnp.concatenate([system, none], axis=0)
@@ -287,14 +353,16 @@
             first_halo(side, q).wait_send()
         for j in range(1, S):
             later_halo(j, side).wait_send()
-    for copy in sent:
-        copy.wait_send()
+    for r in range(2):
+        for f in range(2):
+            for copy in sum_copies(r, f):
+                copy.wait_send()
     for copy in outs:
         copy.wait()
 
 
 def per_device(sizes, blocks, col_index, right_side, start_guess):
-    n_red = sizes[0] - 1 + sizes[1] - 1 + sizes[2] * sizes[3] - 1
+    n_red = sizes[0] - 1 + sizes[1] * sizes[2] * sizes[3] - 1
     anywhere = pl.BlockSpec(memory_space=pltpu.HBM)
     dma = pltpu.SemaphoreType.DMA
     out = jax.ShapeDtypeStruct((NRHS, ROWS * BS), F32)
@@ -314,8 +382,10 @@
             pltpu.VMEM((S, PAIRS, NRHS, 128), F32),
             pltpu.VMEM((PAIRS, 2, S, NRHS, 128), BF16),
             pltpu.VMEM((S, 2, EDGE, NRHS, 128), F32),
-            pltpu.VMEM((3, 32, 128), F32),
-            pltpu.VMEM((n_red, 32, 128), F32),
+            pltpu.VMEM((2, 24, 128), F32),
+            pltpu.VMEM((n_red, 24, 128), F32),
+            pltpu.VMEM((2, 8, 128), F32),
+            pltpu.VMEM((n_red, 8, 128), F32),
             pltpu.VMEM((NRHS, ROWS * BS), F32),
             pltpu.VMEM((NRHS, ROWS * BS), F32),
             dma((ROWS // CHUNK,)),
@@ -324,12 +394,12 @@
             dma((2, EDGE)),
             dma((S - 1, 2)),
             dma((S - 1, 2)),
-            dma((n_red,)),
-            dma((n_red,)),
+            dma((2, n_red)),
+            dma((2, n_red)),
             dma((2, PAIRS // 4)),
         ],
         compiler_params=pltpu.CompilerParams(
-            collective_id=0, has_side_effects=True, vmem_limit_bytes=48 * 1024 * 1024),
+            collective_id=0, has_side_effects=True, vmem_limit_bytes=62 * 1024 * 1024),
         name="gmres_cycle",
     )(col_index.T, blocks, right_side, start_guess)
 

time: 67.5 us -> 52.6 us (0.78)
  Pallas kernels: 62.3 us -> 48.3 us
    pallas_call x1, Pallas kernels: 62.3 us -> 48.3 us  [per_device(): pl.pallas_call(functools.partial(kernel, sizes), out_shape=(out, out), in...]
    unnamed x8 -> x2, local copies, waits for them, and re-layouts: 3.8 us -> 3.14 us
where the time goes in v2:
time: 52.6 us; the launch traced here: 52.1 us
  Pallas kernels  48.3 us (92%)
  local copies, waits for them, and re-layouts  3.14 us (6%)
  between operations  0.64 us (1%)
    pallas_call x1, Pallas kernels, per_device(): pl.pallas_call(functools.partial(kernel, sizes), out_shape=(out, out), in...  48.3 us
    unnamed x2, local copies, waits for them, and re-layouts  3.14 us

profile of v2, /device:TPU:1, one launch (start us, length us, event | category | flops | bytes accessed | tf_op | source)
XLA Modules:
  0.0 52.1 jit_solution(8261291430867573287)
XLA Ops:
  0.6 48.3 %gmres_cycle.1 = (f32[16,2048]{1,0:T(8,128)}, f32[16,2048]{1,0:T(8,128)}) custom-call(s32[8,32]{1,0:T(8,128)} %bitcast.1, f32[32,8,64,64]{3,2,1,0:T(8,128)} %blocks_hbm.1, f32[16,2048]{1,0:T(8,128)} %b_hbm.1, f32[16,2048]{1,0:T(8,128)} %x_hbm.1), custom_call_target="tpu_custom_call" | custom-call | tf_op jit(solution)/shard_map/gmres_cycle/pallas_call | solution.py:369
  48.9 1.6 %copy.8 = f32[16,2048]{1,0:T(8,128)} copy(f32[16,2048]{1,0:T(8,128)} %get-tuple-element.4) | data formatting | bytes 262144
  50.5 1.6 %copy.9 = f32[16,2048]{1,0:T(8,128)} copy(f32[16,2048]{1,0:T(8,128)} %get-tuple-element.5) | data formatting | bytes 262144

commit v3 on v2

--- a/solution.py
+++ b/solution.py
@@ -1,4 +1,5 @@
 import functools
+import itertools
 
 import jax
 import jax.numpy as jnp
@@ -22,6 +23,12 @@
 BF16 = jnp.bfloat16
 
 
+def PHASES(sizes):
+    nz, ny, nx, nc = sizes
+    one = range(1)
+    return ((one, range(ny), range(nx), range(nc)), (range(nz), one, one, one))
+
+
 def split(v):
     high = v.astype(BF16)
     low = (v - high.astype(F32)).astype(BF16)
@@ -43,9 +50,9 @@
     return system
 
 
-def kernel(sizes, col_ref, blocks_hbm, b_hbm, x_hbm, guess_hbm, resid_hbm,
+def kernel(sizes, col_ref, blocks_hbm, b_hbm, x_hbm, guess_hbm,
            at_ref, raw, mat, b_ref, x_ref, vec, dup, basis, halves, halo, early_out, early_in, late_out, late_in,
-           guess, resid, raw_sem, in_sem, halo0_send, halo0_recv, halo_send, halo_recv,
+           guess, raw_sem, in_sem, halo0_send, halo0_recv, halo_send, halo_recv,
            red_send, red_recv, out_sem):
     nz, ny, nx, nc = sizes
     total = nz * ny * nx * nc
@@ -59,14 +66,17 @@
     up = place((linear + 1) % total)
     down = place((linear + total - 1) % total)
 
-    def plane_peer(o):
-        d = ((y * nx + x) * nc + c + o) % (ny * nx * nc)
-        return (z, d // (nx * nc), (d // nc) % nx, d % nc)
-
-    def z_peer(o):
-        return ((z + o) % nz, y, x, c)
-
-    phases = ((ny * nx * nc, plane_peer), (nz, z_peer))
+    def offsets(zs, ys, xs, cs):
+        def hops(d):
+            return sum(min(v, n - v) for v, n in zip(d[:3], (nz, ny, nx)))
+        found = [d for d in itertools.product(zs, ys, xs, cs) if any(d)]
+        return sorted(found, key=lambda d: (-hops(d), d))
+
+    def peer(d):
+        return tuple((v + o) % n for v, o, n in zip(here, d, sizes))
+
+    phases = tuple(offsets(*span) for span in PHASES(sizes))
+    order = jnp.where(linear % (nx * nc) == nx * nc - 1, 1, 0)
 
     def to_remote(src, dst, send, recv, dev):
         return pltpu.make_async_remote_copy(
@@ -77,11 +87,10 @@
     count = 2
     for dev in (up, down):
         pl.semaphore_signal(barrier, inc=1, device_id=dev, device_id_type=pl.DeviceIdType.MESH)
-    for n, peer in phases:
-        for o in range(1, n):
-            count += 1
-            pl.semaphore_signal(barrier, inc=1, device_id=peer(o),
-                                device_id_type=pl.DeviceIdType.MESH)
+    for d in sorted(phases[0] + phases[1], key=lambda d: -sum(min(v, n - v) for v, n in zip(d, sizes))):
+        count += 1
+        pl.semaphore_signal(barrier, inc=1, device_id=peer(d),
+                            device_id_type=pl.DeviceIdType.MESH)
 
     load_x = pltpu.make_async_copy(x_hbm, x_ref, in_sem.at[0])
     load_b = pltpu.make_async_copy(b_hbm, b_ref, in_sem.at[1])
@@ -106,21 +115,22 @@
     lax.fori_loop(0, ROWS, locate, 0)
     pl.semaphore_wait(barrier, count)
 
-    def first_halo(side, q):
-        tile = q if side == 1 else PAIRS - EDGE + q
-        return to_remote(x_hbm.at[:, pl.ds(tile * 128, 128)], halo.at[0, side, q],
-                         halo0_send.at[side, q], halo0_recv.at[side, q],
-                         down if side == 1 else up)
-
-    def later_halo(j, side):
-        start = 0 if side == 1 else PAIRS - EDGE
-        return to_remote(basis.at[j - 1, pl.ds(start, EDGE)], halo.at[j, side],
-                         halo_send.at[j - 1, side], halo_recv.at[j - 1, side],
-                         down if side == 1 else up)
-
-    for q in range(EDGE):
-        for side in range(2):
-            first_halo(side, q).start()
+    def neighbour(w):
+        return tuple(jnp.where(w == 1, u, d) for u, d in zip(up, down))
+
+    def first_halo(w, q):
+        tile = q + w * (PAIRS - EDGE)
+        return to_remote(x_hbm.at[:, pl.ds(pl.multiple_of(tile * 128, 128), 128)],
+                         halo.at[0, 1 - w, q], halo0_send.at[w, q], halo0_recv.at[1 - w, q],
+                         neighbour(w))
+
+    def later_halo(j, w):
+        return to_remote(basis.at[j - 1, pl.ds(w * (PAIRS - EDGE), EDGE)], halo.at[j, 1 - w],
+                         halo_send.at[j - 1, w], halo_recv.at[j - 1, 1 - w], neighbour(w))
+
+    for w in (order, 1 - order):
+        for q in range(EDGE):
+            first_halo(w, q).start()
 
     left = lax.broadcasted_iota(jnp.int32, (NRHS, 128), 1) < BS
     left2 = lax.broadcasted_iota(jnp.int32, (2 * NRHS, 128), 1) < BS
@@ -188,45 +198,38 @@
             halves[p, 0, j] = high
             halves[p, 1, j] = low
 
-    def take_halo(j, side, sign):
+    def take_halo(j, w, sign):
         for q in range(EDGE):
-            v0, v1 = both(sign * halo[j, side, q])
-            row = 2 * q + (0 if side == 0 else BAND + ROWS)
+            v0, v1 = both(sign * halo[j, w, q])
+            row = 2 * q + w * (BAND + ROWS)
             put(j, row, v0)
             put(j, row + 1, v1)
 
-    def wait_first():
-        for side in range(2):
-            for q in range(EDGE):
-                first_halo(side, q).wait_recv()
-
-    def wait_later(j):
-        for side in range(2):
-            later_halo(j, side).wait_recv()
-
-    def edges(j, beta, sign, last):
-        take_halo(j, 0, sign)
-        take_halo(j, 1, sign)
-        for side in (1, 0):
-            start = 0 if side == 1 else PAIRS - EDGE
-            apply_pairs(j, range(start, start + EDGE), beta)
+    def edges(j, beta, sign, first, last):
+        for w in (order, 1 - order):
+            if first is None:
+                later_halo(j, 1 - w).wait_recv()
+            else:
+                @pl.when(first)
+                def _():
+                    for q in range(EDGE):
+                        first_halo(1 - w, q).wait_recv()
+
+                @pl.when(jnp.logical_not(first))
+                def _():
+                    later_halo(j, 1 - w).wait_recv()
+
+            take_halo(j, w, sign)
+            start = w * (PAIRS - EDGE)
+            apply_pairs(j, [start + i for i in range(EDGE)], beta)
             if not last:
-                later_halo(j + 1, side).start()
+                later_halo(j + 1, w).start()
 
     def step(j, _):
         beta = jnp.where(j == 0, 1.0, -2.0)
         sign = jnp.where(j == 0, -1.0, 1.0)
         apply_pairs(j, range(EDGE, PAIRS - EDGE), beta)
-
-        @pl.when(j == 0)
-        def _():
-            wait_first()
-
-        @pl.when(j > 0)
-        def _():
-            wait_later(j)
-
-        edges(j, beta, sign, False)
+        edges(j, beta, sign, j == 0, False)
         return 0
 
     def products(rows, cols, start, n):
@@ -258,15 +261,15 @@
 
     spans = []
     base = 0
-    for n, _ in phases:
-        spans.append((base, n))
-        base += n - 1
+    for phase in phases:
+        spans.append((base, len(phase)))
+        base += len(phase)
 
     def sum_copies(r, f):
         out, inn = (early_out, early_in) if r == 0 else (late_out, late_in)
         base, n = spans[f]
-        return [to_remote(out.at[f], inn.at[base + o - 1], red_send.at[r, base + o - 1],
-                          red_recv.at[r, base + o - 1], phases[f][1](o)) for o in range(1, n)]
+        return [to_remote(out.at[f], inn.at[base + o], red_send.at[r, base + o],
+                          red_recv.at[r, base + o], peer(d)) for o, d in enumerate(phases[f])]
 
     def sum_start(r, f, value):
         (early_out if r == 0 else late_out)[f] = value
@@ -276,9 +279,9 @@
     def sum_finish(r, f, value):
         inn = early_in if r == 0 else late_in
         base, n = spans[f]
-        for o, copy in enumerate(sum_copies(r, f)):
+        for copy in sum_copies(r, f):
             copy.wait_recv()
-        parts = [value] + [inn[base + o] for o in range(n - 1)]
+        parts = [value] + [inn[base + o] for o in range(n)]
         while len(parts) > 1:
             parts = [parts[i] + parts[i + 1] if i + 1 < len(parts) else parts[i]
                      for i in range(0, len(parts), 2)]
@@ -290,9 +293,11 @@
     early = pack(fold(gram))
     sum_start(0, 0, early)
     apply_pairs(S - 1, range(EDGE, PAIRS - EDGE), -2.0)
-    wait_later(S - 1)
-    edges(S - 1, -2.0, 1.0, True)
-    late = pack(fold(products(slice(3, 4), slice(0, 4), 0, PAIRS)))
+    new, every = slice(3, 4), slice(0, 4)
+    inside = products(new, every, EDGE, PAIRS - 2 * EDGE)
+    edges(S - 1, -2.0, 1.0, None, True)
+    late = pack(fold(inside + products(new, every, 0, EDGE)
+                     + products(new, every, PAIRS - EDGE, EDGE)))
     sum_start(1, 0, late)
     early = sum_finish(0, 0, early)
     sum_start(0, 1, early)
@@ -341,18 +346,20 @@
         out = jnp.dot(mix, tile, precision=lax.Precision.HIGHEST, preferred_element_type=F32)
         lanes = slice(p * 128, (p + 4) * 128)
         guess[:, lanes] = x_ref[:, lanes] + out[0:16]
-        resid[:, lanes] = tile[0:16] + out[16:32]
-        for w, (src, dst) in enumerate(((guess, guess_hbm), (resid, resid_hbm))):
+        guess[:, slice(p * 128 + 2048, p * 128 + 2560)] = tile[0:16] + out[16:32]
+        for w in range(2):
+            src, dst = guess, guess_hbm
+            lanes = slice(p * 128 + w * 2048, p * 128 + w * 2048 + 512)
             copy = pltpu.make_async_copy(src.at[:, lanes], dst.at[:, lanes],
                                          out_sem.at[w, p // 4])
             copy.start()
             outs.append(copy)
 
-    for side in range(2):
+    for w in range(2):
         for q in range(EDGE):
-            first_halo(side, q).wait_send()
+            first_halo(w, q).wait_send()
         for j in range(1, S):
-            later_halo(j, side).wait_send()
+            later_halo(j, w).wait_send()
     for r in range(2):
         for f in range(2):
             for copy in sum_copies(r, f):
@@ -362,15 +369,15 @@
 
 
 def per_device(sizes, blocks, col_index, right_side, start_guess):
-    n_red = sizes[0] - 1 + sizes[1] * sizes[2] * sizes[3] - 1
+    n_red = sum(len(z) * len(y) * len(x) * len(c) - 1 for z, y, x, c in PHASES(sizes))
     anywhere = pl.BlockSpec(memory_space=pltpu.HBM)
     dma = pltpu.SemaphoreType.DMA
     out = jax.ShapeDtypeStruct((NRHS, ROWS * BS), F32)
-    return pl.pallas_call(
+    out = pl.pallas_call(
         functools.partial(kernel, sizes),
-        out_shape=(out, out),
+        out_shape=jax.ShapeDtypeStruct((NRHS, 2 * ROWS * BS), F32),
         in_specs=[pl.BlockSpec(memory_space=pltpu.SMEM), anywhere, anywhere, anywhere],
-        out_specs=(anywhere, anywhere),
+        out_specs=anywhere,
         scratch_shapes=[
             pltpu.SMEM((NNZB, ROWS), jnp.int32),
             pltpu.VMEM((ROWS, NNZB, BS, BS), F32),
@@ -386,8 +393,7 @@
             pltpu.VMEM((n_red, 24, 128), F32),
             pltpu.VMEM((2, 8, 128), F32),
             pltpu.VMEM((n_red, 8, 128), F32),
-            pltpu.VMEM((NRHS, ROWS * BS), F32),
-            pltpu.VMEM((NRHS, ROWS * BS), F32),
+            pltpu.VMEM((NRHS, 2 * ROWS * BS), F32),
             dma((ROWS // CHUNK,)),
             dma((2,)),
             dma((2, EDGE)),
@@ -402,6 +408,7 @@
             collective_id=0, has_side_effects=True, vmem_limit_bytes=62 * 1024 * 1024),
         name="gmres_cycle",
     )(col_index.T, blocks, right_side, start_guess)
+    return out[:, :ROWS * BS], out[:, ROWS * BS:]
 
 
 def solution(mesh, sizes=(8, 4, 4, 2)):

time: 52.6 us -> 50.6 us (0.962)
  local copies, waits for them, and re-layouts: 3.14 us -> 1.69 us
  Pallas kernels: 48.3 us -> 47.5 us
    unnamed x2 -> x0, local copies, waits for them, and re-layouts: 3.14 us -> none
    slice x0 -> x1, local copies, waits for them, and re-layouts: none -> 1.69 us  [per_device(): return (out[:, :ROWS * BS], out[:, ROWS * BS:])]
    pallas_call x1, Pallas kernels: 48.3 us -> 47.5 us  [per_device(): pl.pallas_call(functools.partial(kernel, sizes), out_shape=jax.ShapeDtype...]
where the time goes in v3:
time: 50.6 us; the launch traced here: 49.8 us
  Pallas kernels  47.5 us (94%)
  local copies, waits for them, and re-layouts  1.69 us (3%)
  between operations  0.64 us (1%)
    pallas_call x1, Pallas kernels, per_device(): pl.pallas_call(functools.partial(kernel, sizes), out_shape=jax.ShapeDtype...  47.5 us
    slice x1, local copies, waits for them, and re-layouts, per_device(): return (out[:, :ROWS * BS], out[:, ROWS * BS:])  1.69 us

profile of v3, /device:TPU:1, one launch (start us, length us, event | category | flops | bytes accessed | tf_op | source)
XLA Modules:
  0.0 49.8 jit_solution(12708280539507672034)
XLA Ops:
  0.6 47.5 %gmres_cycle.1 = f32[16,4096]{1,0:T(8,128)} custom-call(s32[8,32]{1,0:T(8,128)} %bitcast.1, f32[32,8,64,64]{3,2,1,0:T(8,128)} %blocks_hbm.1, f32[16,2048]{1,0:T(8,128)} %b_hbm.1, f32[16,2048]{1,0:T(8,128)} %x_hbm.1), custom_call_target="tpu_custom_call" | custom-call | tf_op jit(solution)/shard_map/gmres_cycle/pallas_call | solution.py:376
  48.1 1.7 %fusion = (f32[16,2048]{1,0:T(8,128)}, f32[16,2048]{1,0:T(8,128)}) fusion(f32[16,4096]{1,0:T(8,128)} %gmres_cycle.1), kind=kLoop, calls=%fused_computation | loop fusion | bytes 524288 | tf_op jit(solution)/shard_map/slice | solution.py:411

commit v4 on v3

--- a/solution.py
+++ b/solution.py
@@ -10,6 +10,7 @@
 from jax.sharding import PartitionSpec as P
 
 BS = 64
+STEPS = 4
 NNZB = 8
 NRHS = 16
 S = 4
@@ -42,11 +43,30 @@
 def eliminate(system, start, n):
     rows = system.shape[0]
     sub = lax.broadcasted_iota(jnp.int32, system.shape, 0)
-    for k in range(start, start + n):
-        row = jnp.broadcast_to(system[k:k + 1, :], system.shape)
-        col = jnp.broadcast_to(system[:, k:k + 1], system.shape)
-        scaled = row * (1.0 / jnp.broadcast_to(system[k:k + 1, k:k + 1], (1, 128)))
-        system = jnp.where(sub == k, scaled, system - col * scaled)
+    for k in range(start, start + n, STEPS):
+        cols = [jnp.broadcast_to(system[:, k + i:k + i + 1], system.shape) for i in range(STEPS)]
+        rows = []
+        for i in range(STEPS):
+            row = system[k + i:k + i + 1]
+            lead = [cols[m][k + i:k + i + 1] for m in range(STEPS)]
+            rows.append((row, lead))
+        done = [r for r, _ in rows]
+        lead = [l for _, l in rows]
+        for i in range(STEPS):
+            inv = 1.0 / lead[i][i]
+            done[i] = done[i] * inv
+            lead[i] = [v * inv for v in lead[i]]
+            for m in range(STEPS):
+                if m != i:
+                    factor = lead[m][i]
+                    done[m] = done[m] - factor * done[i]
+                    lead[m] = [a - factor * b for a, b in zip(lead[m], lead[i])]
+        block = system
+        for i in range(STEPS):
+            block = block - cols[i] * done[i]
+        for i in range(STEPS):
+            block = jnp.where(sub == k + i, done[i], block)
+        system = block
     return system
 
 
@@ -279,13 +299,11 @@
     def sum_finish(r, f, value):
         inn = early_in if r == 0 else late_in
         base, n = spans[f]
-        for copy in sum_copies(r, f):
-            copy.wait_recv()
-        parts = [value] + [inn[base + o] for o in range(n)]
-        while len(parts) > 1:
-            parts = [parts[i] + parts[i + 1] if i + 1 < len(parts) else parts[i]
-                     for i in range(0, len(parts), 2)]
-        return parts[0]
+        copies = sum_copies(r, f)
+        for o in reversed(range(n)):
+            copies[o].wait_recv()
+            value = value + inn[base + o]
+        return value
 
     lax.fori_loop(0, S - 1, step, 0)
     halves[:, :, S - 1] = jnp.zeros((PAIRS, 2, NRHS, 128), BF16)
@@ -313,6 +331,13 @@
     system = jnp.where(lane32 < 64, system, jnp.where(lane32 - 64 == sub32, 1.0, 0.0))
     system = eliminate(system, 0, 32)
 
+    for w in range(2):
+        for q in range(EDGE):
+            first_halo(w, q).wait_send()
+        for j in range(1, S):
+            later_halo(j, w).wait_send()
+    for copy in sum_copies(0, 0) + sum_copies(0, 1) + sum_copies(1, 0):
+        copy.wait_send()
     late = unpack(sum_finish(1, 1, late))
     lane16 = lax.broadcasted_iota(jnp.int32, (16, 128), 1)
     turned = jnp.transpose(jnp.concatenate([late, jnp.zeros((112, 128), F32)], axis=0))
@@ -355,15 +380,8 @@
             copy.start()
             outs.append(copy)
 
-    for w in range(2):
-        for q in range(EDGE):
-            first_halo(w, q).wait_send()
-        for j in range(1, S):
-            later_halo(j, w).wait_send()
-    for r in range(2):
-        for f in range(2):
-            for copy in sum_copies(r, f):
-                copy.wait_send()
+    for copy in sum_copies(1, 1):
+        copy.wait_send()
     for copy in outs:
         copy.wait()
 

time: 50.6 us -> 49.9 us (0.986)
  Pallas kernels: 47.5 us -> 46.7 us
    pallas_call x1, Pallas kernels: 47.5 us -> 46.7 us  [per_device(): pl.pallas_call(functools.partial(kernel, sizes), out_shape=jax.ShapeDtype...]
where the time goes in v4:
time: 49.9 us; the launch traced here: 49 us
  Pallas kernels  46.7 us (94%)
  local copies, waits for them, and re-layouts  1.69 us (3%)
  between operations  0.64 us (1%)
    pallas_call x1, Pallas kernels, per_device(): pl.pallas_call(functools.partial(kernel, sizes), out_shape=jax.ShapeDtype...  46.7 us
    slice x1, local copies, waits for them, and re-layouts, per_device(): return (out[:, :ROWS * BS], out[:, ROWS * BS:])  1.69 us

profile of v4, /device:TPU:1, one launch (start us, length us, event | category | flops | bytes accessed | tf_op | source)
XLA Modules:
  0.0 49.0 jit_solution(890114222224006457)
XLA Ops:
  0.6 46.7 %gmres_cycle.1 = f32[16,4096]{1,0:T(8,128)} custom-call(s32[8,32]{1,0:T(8,128)} %bitcast.1, f32[32,8,64,64]{3,2,1,0:T(8,128)} %blocks_hbm.1, f32[16,2048]{1,0:T(8,128)} %b_hbm.1, f32[16,2048]{1,0:T(8,128)} %x_hbm.1), custom_call_target="tpu_custom_call" | custom-call | tf_op jit(solution)/shard_map/gmres_cycle/pallas_call | solution.py:394
  47.3 1.7 %fusion = (f32[16,2048]{1,0:T(8,128)}, f32[16,2048]{1,0:T(8,128)}) fusion(f32[16,4096]{1,0:T(8,128)} %gmres_cycle.1), kind=kLoop, calls=%fused_computation | loop fusion | bytes 524288 | tf_op jit(solution)/shard_map/slice | solution.py:429

commit v5 on v4

--- a/solution.py
+++ b/solution.py
@@ -309,10 +309,10 @@
     halves[:, :, S - 1] = jnp.zeros((PAIRS, 2, NRHS, 128), BF16)
     gram = products(slice(0, 3), slice(0, 4), 0, PAIRS)
     early = pack(fold(gram))
-    sum_start(0, 0, early)
     apply_pairs(S - 1, range(EDGE, PAIRS - EDGE), -2.0)
     new, every = slice(3, 4), slice(0, 4)
     inside = products(new, every, EDGE, PAIRS - 2 * EDGE)
+    sum_start(0, 0, early)
     edges(S - 1, -2.0, 1.0, None, True)
     late = pack(fold(inside + products(new, every, 0, EDGE)
                      + products(new, every, PAIRS - EDGE, EDGE)))

time: 49.9 us -> 49.7 us (level)
  no operation moved by 1% of the time
where the time goes in v5:
time: 49.7 us; the launch traced here: 48.7 us
  Pallas kernels  46.4 us (93%)
  local copies, waits for them, and re-layouts  1.69 us (3%)
  between operations  0.64 us (1%)
    pallas_call x1, Pallas kernels, per_device(): pl.pallas_call(functools.partial(kernel, sizes), out_shape=jax.ShapeDtype...  46.4 us
    slice x1, local copies, waits for them, and re-layouts, per_device(): return (out[:, :ROWS * BS], out[:, ROWS * BS:])  1.69 us

profile of v5, /device:TPU:1, one launch (start us, length us, event | category | flops | bytes accessed | tf_op | source)
XLA Modules:
  0.0 48.7 jit_solution(7856503938324155950)
XLA Ops:
  0.6 46.4 %gmres_cycle.1 = f32[16,4096]{1,0:T(8,128)} custom-call(s32[8,32]{1,0:T(8,128)} %bitcast.1, f32[32,8,64,64]{3,2,1,0:T(8,128)} %blocks_hbm.1, f32[16,2048]{1,0:T(8,128)} %b_hbm.1, f32[16,2048]{1,0:T(8,128)} %x_hbm.1), custom_call_target="tpu_custom_call" | custom-call | tf_op jit(solution)/shard_map/gmres_cycle/pallas_call | solution.py:394
  47.0 1.7 %fusion = (f32[16,2048]{1,0:T(8,128)}, f32[16,2048]{1,0:T(8,128)}) fusion(f32[16,4096]{1,0:T(8,128)} %gmres_cycle.1), kind=kLoop, calls=%fused_computation | loop fusion | bytes 524288 | tf_op jit(solution)/shard_map/slice | solution.py:429
